TPU v7x, 32 devices: a whole 2x2x4 slice. The times are simulated.
32 devices in a mesh: shard: 2 (over y), ctx: 4 (over z), tp: 4 (over x, core).
Axes of the slice: x: 2, y: 2, z: 4, core: 2. Of those that a mesh axis runs over, the one named last changes fastest.
Arguments:
- x_in: float32 [4096, 768], P(('shard', 'ctx')), may hold values from -6 to 6
- norm_gain: bfloat16 [768], P(('shard', 'ctx')), may hold values from 0.5 to 1.5
- w_z: bfloat16 [768, 1536], P(('shard', 'ctx'), 'tp'), may hold values from -0.21875 to 0.21875
- w_x: bfloat16 [768, 1536], P(('shard', 'ctx'), 'tp'), may hold values from -0.21875 to 0.21875
- w_bc: bfloat16 [768, 256], P(('shard', 'ctx')), may hold values from -0.21875 to 0.21875
- w_dt: bfloat16 [768, 24], P(('shard', 'ctx'), 'tp'), may hold values from -0.21875 to 0.21875
- w_out: bfloat16 [768, 1536], P(('shard', 'ctx'), 'tp'), may hold values from -0.15625 to 0.15625
- conv_wx: float32 [4, 1536], P(None, 'tp'), may hold values from -3 to 3
- conv_bx: float32 [1536], P('tp'), may hold values from -0.5 to 0.5
- conv_wbc: float32 [4, 256], replicated, may hold values from -3 to 3
- conv_bbc: float32 [256], replicated, may hold values from -0.5 to 0.5
- dt_bias: float32 [24], P('tp'), may hold values from -6 to -3
- a_log: float32 [24], P('tp'), may hold values from -6 to 2
- d_skip: float32 [24], P('tp'), may hold values from 0.5 to 1.5
- gate_gain: float32 [1536], P('tp'), may hold values from 0.5 to 1.5
- seq_lens: int32 [2, 3], P('shard'), may hold values from 1 to 1280, 2048 in all within a row
- token_mask: int32 [4096], P(('shard', 'ctx')), may hold values 0 or 1
- d_out: float32 [4096, 768], P(('shard', 'ctx')), may hold values from -6 to 6
Outputs:
- block_out: float32 [4096, 768], P(('shard', 'ctx'))
- d_x: float32 [4096, 768], P(('shard', 'ctx'))
- d_norm_gain: float32 [768], P(('shard', 'ctx'))
- d_w_z: float32 [768, 1536], P(('shard', 'ctx'), 'tp')
- d_w_x: float32 [768, 1536], P(('shard', 'ctx'), 'tp')
- d_w_bc: float32 [768, 256], P(('shard', 'ctx'))
- d_w_dt: float32 [768, 24], P(('shard', 'ctx'), 'tp')
- d_w_out: float32 [768, 1536], P(('shard', 'ctx'), 'tp')
- d_conv_wx: float32 [4, 1536], P(None, 'tp')
- d_conv_bx: float32 [1536], P('tp')
- d_conv_wbc: float32 [4, 256], replicated
- d_conv_bbc: float32 [256], replicated
- d_dt_bias: float32 [24], P('tp')
- d_a_log: float32 [24], P('tp')
- d_d_skip: float32 [24], P('tp')
- d_gate_gain: float32 [1536], P('tp')
Inputs may be any that keep to these rules, and one draw needn't show every extreme that they name: `seq_lens`: each row sums to 2048, and its longest sequence has exactly 1280 positions.
All inputs are finite; a program needn't handle non-finite values. No bound on the sum of `token_mask` on one device may be relied on, other than what follows from the above.
Results may differ from a plain program's by a relative error of at most 0.014.
Values may be sent and summed in bfloat16 or wider, within the bound.
No kernel may reach another device: no remote copies, remote signals or barrier semaphores. Data moves between devices by JAX's collectives and lax.ppermute only.
A program may use at most 128 MiB of HBM per device.

v0:
```python
import jax
import jax.numpy as jnp
from jax import lax
from jax.sharding import PartitionSpec as P

SPAN = 256
norm_eps = 1e-05


def passed_along(value, axis, steps):
    count = lax.axis_size(axis)
    initial, last = (max(0, -steps), min(count, count - steps))
    return lax.ppermute(value, axis, [(source, source + steps) for source in range(initial, last)])


def entering_2(part, axis, combine, identity, reverse):
    count = lax.axis_size(axis)
    place = lax.axis_index(axis)
    ahead = count - 1 - place if reverse else place
    gathered = jax.tree.map(lambda a: lax.all_gather(a, axis), part)
    state = jax.tree.map(lambda a, e: jnp.zeros_like(a) + jnp.asarray(e, a.dtype), part, identity)

    def one(step, state):
        source = count - 1 - step if reverse else step
        return combine(
            state, jax.tree.map(lambda a: lax.dynamic_index_in_dim(a, source, 0, False), gathered)
        )

    return lax.fori_loop(0, ahead, one, state)


def segment_ids(positions, lengths_row):
    bounds = jnp.cumsum(lengths_row)
    counted = jnp.sum((positions[:, None] >= bounds[None, :]).astype(jnp.int32), axis=1)
    return jnp.where(positions < 0, -1, counted)


def conv_silu(extended, seg_ext, weight, conv_bias):
    width_taps = weight.shape[0]
    row_count = extended.shape[0] - (width_taps - 1)
    summed = jnp.zeros((row_count, extended.shape[1]), jnp.float32) + conv_bias[None, :]
    for offset in range(width_taps):
        same_doc = (seg_ext[offset : offset + row_count] == seg_ext[width_taps - 1 :]).astype(
            jnp.float32
        )
        summed = (
            summed
            + weight[offset][None, :] * extended[offset : offset + row_count] * same_doc[:, None]
        )
    return jax.nn.silu(summed)


def span_output(ssm_in, step_size, decay_rate, b_state, c_state, segment, seg_prev, state_in):
    cumulated = jnp.cumsum(step_size * decay_rate[None, :], axis=0)
    length = ssm_in.shape[0]
    ordering = jnp.arange(length, dtype=jnp.int32)
    allowed = (segment[:, None] == segment[None, :]) & (ordering[:, None] >= ordering[None, :])
    log_gaps = cumulated[:, None, :] - cumulated[None, :, :]
    log_gaps = jnp.where(allowed[:, :, None], log_gaps, 0.0)
    decays = jnp.where(allowed[:, :, None], jnp.exp(log_gaps), 0.0)
    scores = lax.dot_general(
        c_state, b_state, (((1,), (1,)), ((), ())), precision=lax.Precision.HIGHEST
    )
    mixing = scores[:, :, None] * decays * step_size[None, :, :]
    within = jnp.einsum("tsh,shp->thp", mixing, ssm_in, precision=lax.Precision.HIGHEST)
    carried = jnp.einsum("tn,hpn->thp", c_state, state_in, precision=lax.Precision.HIGHEST)
    entering = jnp.exp(cumulated) * (segment == seg_prev).astype(jnp.float32)[:, None]
    return within + carried * entering[:, :, None]


def span_state(ssm_in, step_size, decay_rate, b_state, segment, seg_prev):
    cumulated = jnp.cumsum(step_size * decay_rate[None, :], axis=0)
    final_sum = cumulated[-1]
    kept = (segment == segment[-1])[:, None]
    remaining = jnp.where(kept, final_sum[None, :] - cumulated, 0.0)
    weighting = jnp.where(kept, jnp.exp(remaining) * step_size, 0.0)
    scaled_in = ssm_in * weighting[:, :, None]
    state_out = jnp.einsum("shp,sn->hpn", scaled_in, b_state, precision=lax.Precision.HIGHEST)
    passing = jnp.exp(final_sum) * (segment[-1] == seg_prev).astype(jnp.float32)
    return (passing, state_out)


def forward_join(earlier, later):
    return (earlier[0] * later[0], later[0][:, None, None] * earlier[1] + later[1])


def backward_join(earlier, later):
    return (earlier[0] * later[0], later[1] + later[0][:, None, None] * earlier[1])


def contract_rows(left_side, right_side):
    return lax.dot_general(
        left_side, right_side, (((0,), (0,)), ((), ())), preferred_element_type=jnp.float32
    )


def contract_cols(left_side, right_side):
    return lax.dot_general(
        left_side, right_side, (((1,), (1,)), ((), ())), preferred_element_type=jnp.float32
    )


def local(
    x_in,
    norm_gain,
    w_z,
    w_x,
    w_bc,
    w_dt,
    w_out,
    conv_wx,
    conv_bx,
    conv_wbc,
    conv_bbc,
    dt_bias,
    a_log,
    d_skip,
    gate_gain,
    seq_lens,
    token_mask,
    d_out,
):
    row_count = x_in.shape[0]
    head_count = dt_bias.shape[0]
    inner_local = w_z.shape[1]
    head_width = inner_local // head_count
    state_width = w_bc.shape[1] // 2
    edge_rows = conv_wx.shape[0] - 1
    span_count = row_count // SPAN
    tp_count = lax.axis_size("tp")
    inner_total = inner_local * tp_count
    gathered = (
        lax.all_gather(norm_gain, ("shard", "ctx"), axis=0, tiled=True),
        lax.all_gather(w_z, ("shard", "ctx"), axis=0, tiled=True),
        lax.all_gather(w_x, ("shard", "ctx"), axis=0, tiled=True),
        lax.all_gather(w_bc, ("shard", "ctx"), axis=0, tiled=True),
        lax.all_gather(w_dt, ("shard", "ctx"), axis=0, tiled=True),
        lax.all_gather(w_out, ("shard", "ctx"), axis=0, tiled=True),
    )
    gain_all, wz_all, wx_all, wbc_all, wdt_all, wout_all = gathered
    inv_rms = lax.rsqrt(jnp.mean(x_in * x_in, axis=1, keepdims=True) + norm_eps)
    normed = (x_in * inv_rms * gain_all[None, :]).astype(jnp.bfloat16)
    proj_z = jnp.dot(normed, wz_all, preferred_element_type=jnp.float32).astype(jnp.bfloat16)
    proj_x = jnp.dot(normed, wx_all, preferred_element_type=jnp.float32).astype(jnp.bfloat16)
    proj_bc = jnp.dot(normed, wbc_all, preferred_element_type=jnp.float32).astype(jnp.bfloat16)
    proj_dt = jnp.dot(normed, wdt_all, preferred_element_type=jnp.float32).astype(jnp.bfloat16)
    conv_input = jnp.concatenate([proj_x, proj_bc], axis=1)
    edge_in = passed_along(conv_input[row_count - edge_rows :], "ctx", 1)
    extended = jnp.concatenate([edge_in, conv_input], axis=0).astype(jnp.float32)
    positions = lax.axis_index("ctx") * row_count + jnp.arange(
        -edge_rows, row_count, dtype=jnp.int32
    )
    seg_ext = segment_ids(positions, seq_lens[0])
    segment = seg_ext[edge_rows:]
    seg_prev = seg_ext[edge_rows - 1 : edge_rows - 1 + row_count : SPAN]
    conv_w = jnp.concatenate([conv_wx, conv_wbc], axis=1)
    conv_b = jnp.concatenate([conv_bx, conv_bbc])

    def conv_piece(ext_arg, weight_arg, bias_arg):
        return conv_silu(ext_arg, seg_ext, weight_arg, bias_arg)

    activated, conv_back = jax.vjp(conv_piece, extended, conv_w, conv_b)
    ssm_in = activated[:, :inner_local].reshape(row_count, head_count, head_width)
    b_state = activated[:, inner_local : inner_local + state_width]
    c_state = activated[:, inner_local + state_width :]
    mask_f = token_mask.astype(jnp.float32)
    dt_pre = proj_dt.astype(jnp.float32) + dt_bias[None, :]
    step_size = jax.nn.softplus(dt_pre) * mask_f[:, None]
    decay_rate = -jnp.exp(a_log)
    span_in = ssm_in.reshape(span_count, SPAN, head_count, head_width)
    span_dt = step_size.reshape(span_count, SPAN, head_count)
    span_b = b_state.reshape(span_count, SPAN, state_width)
    span_c = c_state.reshape(span_count, SPAN, state_width)
    span_seg = segment.reshape(span_count, SPAN)

    def states_call(in_arg, dt_arg, rate_arg, b_arg):
        return jax.vmap(span_state, in_axes=(0, 0, None, 0, 0, 0))(
            in_arg, dt_arg, rate_arg, b_arg, span_seg, seg_prev
        )

    (passing, local_states), state_back = jax.vjp(states_call, span_in, span_dt, decay_rate, span_b)
    ones_head = jnp.ones((head_count,), jnp.float32)
    zeros_state = jnp.zeros((head_count, head_width, state_width), jnp.float32)
    dev_pass, dev_state = (ones_head, zeros_state)
    for span_index in range(span_count):
        dev_pass, dev_state = forward_join(
            (dev_pass, dev_state), (passing[span_index], local_states[span_index])
        )
    state_entry = entering_2(
        (dev_pass, dev_state), "ctx", forward_join, (ones_head, zeros_state), False
    )[1]
    entries = []
    current = state_entry
    for span_index in range(span_count):
        entries.append(current)
        current = passing[span_index][:, None, None] * current + local_states[span_index]
    span_entry = jnp.stack(entries)

    def outputs_call(in_arg, dt_arg, rate_arg, b_arg, c_arg, entry_arg):
        return jax.vmap(span_output, in_axes=(0, 0, None, 0, 0, 0, 0, 0))(
            in_arg, dt_arg, rate_arg, b_arg, c_arg, span_seg, seg_prev, entry_arg
        )

    span_out, output_back = jax.vjp(
        outputs_call, span_in, span_dt, decay_rate, span_b, span_c, span_entry
    )
    ssm_out = span_out.reshape(row_count, head_count, head_width) + d_skip[None, :, None] * ssm_in
    ssm_flat = ssm_out.reshape(row_count, inner_local)
    z_float = proj_z.astype(jnp.float32)
    gate_act = jax.nn.silu(z_float)
    gated = ssm_flat * gate_act
    square_sum = lax.psum(jnp.sum(gated * gated, axis=1), "tp")
    inv_gate = lax.rsqrt(square_sum / inner_total + norm_eps)
    mixed = (gated * inv_gate[:, None] * gate_gain[None, :]).astype(jnp.bfloat16)
    block_out = x_in + lax.psum(contract_cols(mixed, wout_all), "tp")
    weights_back = (
        lax.all_gather(norm_gain, ("shard", "ctx"), axis=0, tiled=True),
        lax.all_gather(w_z, ("shard", "ctx"), axis=0, tiled=True),
        lax.all_gather(w_x, ("shard", "ctx"), axis=0, tiled=True),
        lax.all_gather(w_bc, ("shard", "ctx"), axis=0, tiled=True),
        lax.all_gather(w_dt, ("shard", "ctx"), axis=0, tiled=True),
        lax.all_gather(w_out, ("shard", "ctx"), axis=0, tiled=True),
    )
    gain_back, wz_back, wx_back, wbc_back, wdt_back, wout_back = weights_back
    grad_low = d_out.astype(jnp.bfloat16)
    d_mixed = jnp.dot(grad_low, wout_back, preferred_element_type=jnp.float32)
    d_w_out = contract_rows(grad_low, mixed)
    scaled = d_mixed * gate_gain[None, :]
    back_dot = lax.psum(jnp.sum(scaled * gated, axis=1), "tp")
    d_gated = (
        scaled * inv_gate[:, None]
        - gated * (inv_gate * inv_gate * inv_gate * back_dot / inner_total)[:, None]
    )
    d_gate_gain = jnp.sum(d_mixed * gated * inv_gate[:, None], axis=0)
    sigmoid_z = jax.nn.sigmoid(z_float)
    d_z = d_gated * ssm_flat * sigmoid_z * (1.0 + z_float * (1.0 - sigmoid_z))
    d_ssm = (d_gated * gate_act).reshape(row_count, head_count, head_width)
    d_d_skip = jnp.sum(d_ssm * ssm_in, axis=(0, 2))
    g_in, g_dt, g_rate, g_b, g_c, g_entry = output_back(
        d_ssm.reshape(span_count, SPAN, head_count, head_width)
    )
    back_pass, back_grad = (ones_head, zeros_state)
    for span_index in reversed(range(span_count)):
        back_pass, back_grad = backward_join(
            (back_pass, back_grad), (passing[span_index], g_entry[span_index])
        )
    exit_grad = entering_2(
        (back_pass, back_grad), "ctx", backward_join, (ones_head, zeros_state), True
    )[1]
    next_grad = exit_grad
    pass_list = []
    state_list = []
    for span_index in reversed(range(span_count)):
        pass_list.append(jnp.sum(next_grad * span_entry[span_index], axis=(1, 2)))
        state_list.append(next_grad)
        next_grad = g_entry[span_index] + passing[span_index][:, None, None] * next_grad
    s_in, s_dt, s_rate, s_b = state_back((jnp.stack(pass_list[::-1]), jnp.stack(state_list[::-1])))
    d_in_total = (
        d_ssm * d_skip[None, :, None] + (g_in + s_in).reshape(row_count, head_count, head_width)
    ).reshape(row_count, inner_local)
    d_step = (g_dt + s_dt).reshape(row_count, head_count)
    d_a_log = (g_rate + s_rate) * decay_rate
    d_dt_pre = d_step * mask_f[:, None] * jax.nn.sigmoid(dt_pre)
    d_dt_bias = jnp.sum(d_dt_pre, axis=0)
    d_bc = lax.psum(
        jnp.concatenate(
            [(g_b + s_b).reshape(row_count, state_width), g_c.reshape(row_count, state_width)],
            axis=1,
        ),
        "tp",
    )
    d_ext, d_conv_w, d_conv_b = conv_back(jnp.concatenate([d_in_total, d_bc], axis=1))
    edge_grad = passed_along(d_ext[:edge_rows], "ctx", -1)
    d_conv_in = d_ext[edge_rows:] + jnp.concatenate(
        [jnp.zeros((row_count - edge_rows, d_ext.shape[1]), jnp.float32), edge_grad], axis=0
    )
    d_proj_z = d_z.astype(jnp.bfloat16)
    d_proj_x = d_conv_in[:, :inner_local].astype(jnp.bfloat16)
    d_proj_bc = d_conv_in[:, inner_local:].astype(jnp.bfloat16)
    d_proj_dt = d_dt_pre.astype(jnp.bfloat16)
    d_w_z = contract_rows(normed, d_proj_z)
    d_w_x = contract_rows(normed, d_proj_x)
    d_w_bc = contract_rows(normed, d_proj_bc)
    d_w_dt = contract_rows(normed, d_proj_dt)
    share = 2 * state_width // tp_count
    share_start = lax.axis_index("tp") * share
    bc_part = lax.dynamic_slice_in_dim(d_proj_bc, share_start, share, 1)
    wbc_part = lax.dynamic_slice_in_dim(wbc_back, share_start, share, 1)
    d_normed_part = (
        contract_cols(d_proj_z, wz_back)
        + contract_cols(d_proj_x, wx_back)
        + contract_cols(d_proj_dt, wdt_back)
        + contract_cols(bc_part, wbc_part)
    )
    d_normed = lax.psum(d_normed_part, "tp")
    gain_float = gain_back.astype(jnp.float32)
    weighted = d_normed * gain_float[None, :]
    row_dot = jnp.sum(weighted * x_in, axis=1, keepdims=True)
    d_input = (
        d_out + weighted * inv_rms - x_in * (inv_rms * inv_rms * inv_rms) * row_dot / x_in.shape[1]
    )
    d_norm_gain = jnp.sum(d_normed * x_in * inv_rms, axis=0)
    grads_rows = (
        lax.psum_scatter(d_norm_gain, ("shard", "ctx"), scatter_dimension=0, tiled=True),
        lax.psum_scatter(d_w_z, ("shard", "ctx"), scatter_dimension=0, tiled=True),
        lax.psum_scatter(d_w_x, ("shard", "ctx"), scatter_dimension=0, tiled=True),
        lax.psum_scatter(d_w_bc, ("shard", "ctx"), scatter_dimension=0, tiled=True),
        lax.psum_scatter(d_w_dt, ("shard", "ctx"), scatter_dimension=0, tiled=True),
        lax.psum_scatter(d_w_out, ("shard", "ctx"), scatter_dimension=0, tiled=True),
    )
    grads_small = lax.psum(
        (
            d_conv_w[:, :inner_local],
            d_conv_b[:inner_local],
            d_conv_w[:, inner_local:],
            d_conv_b[inner_local:],
            d_dt_bias,
            d_a_log,
            d_d_skip,
            d_gate_gain,
        ),
        ("shard", "ctx"),
    )
    return (block_out, d_input) + tuple(grads_rows) + tuple(grads_small)


def solution(mesh):
    in_specs = (
        P(("shard", "ctx"), None),
        P(("shard", "ctx")),
        P(("shard", "ctx"), "tp"),
        P(("shard", "ctx"), "tp"),
        P(("shard", "ctx"), None),
        P(("shard", "ctx"), "tp"),
        P(("shard", "ctx"), "tp"),
        P(None, "tp"),
        P("tp"),
        P(),
        P(),
        P("tp"),
        P("tp"),
        P("tp"),
        P("tp"),
        P("shard", None),
        P(("shard", "ctx")),
        P(("shard", "ctx"), None),
    )
    out_specs = (
        P(("shard", "ctx"), None),
        P(("shard", "ctx"), None),
        P(("shard", "ctx")),
        P(("shard", "ctx"), "tp"),
        P(("shard", "ctx"), "tp"),
        P(("shard", "ctx"), None),
        P(("shard", "ctx"), "tp"),
        P(("shard", "ctx"), "tp"),
        P(None, "tp"),
        P("tp"),
        P(),
        P(),
        P("tp"),
        P("tp"),
        P("tp"),
        P("tp"),
    )
    return jax.shard_map(local, mesh=mesh, in_specs=in_specs, out_specs=out_specs, check_vma=False)
```

profile of v0, /device:TPU:0, one launch (start us, length us, event | category | flops | bytes accessed | tf_op | source)
XLA Modules:
  0.0 740.0 jit_solution(11802772504556796452)
XLA Ops:
  11.0 23.3 %all-reduce.10 = bf16[768]{0:T(1024)(128)(2,1)S(1)} all-reduce(bf16[768]{0:T(1024)(128)(2,1)S(1)} %dynamic-update-slice), channel_id=1, replica_groups=mesh['shard'=2,'ctx'=4,'tp'=4] {'shard','ctx'}, use_global_device_ids=true, to_apply=%add.10 | all-reduce | flops 768 | bytes 3072
  34.3 1.6 multiply_reduce_fusion.3
  36.5 33.1 %all_gather.19 = bf16[768,384]{1,0:T(8,128)(2,1)S(1)} all-gather(bf16[96,384]{1,0:T(8,128)(2,1)} %param.25), channel_id=1, replica_groups=mesh['shard'=2,'ctx'=4,'tp'=4] {'shard','ctx'}, dimensions={0}, use_global_device_ids=true | all-gather | bytes 663552 | tf_op jit(solution)/shard_map/all_gather | solution.py:135
  69.5 31.4 %all_gather.40 = bf16[768,256]{1,0:T(8,128)(2,1)S(1)} all-gather(bf16[96,256]{1,0:T(8,128)(2,1)S(1)} %copy-done.60), channel_id=1, replica_groups=mesh['shard'=2,'ctx'=4,'tp'=4] {'shard','ctx'}, dimensions={0}, use_global_device_ids=true | all-gather | bytes 442368 | tf_op jit(solution)/shard_map/all_gather | solution.py:136
  102.5 1.4 collective-permute-start
  105.3 27.0 %all-gather = bf16[8,96,6]{1,2,0:T(8,128)(2,1)S(1)} all-gather(bf16[1,96,6]{1,2,0:T(8,128)(2,1)S(1)} %bitcast.232), channel_id=1, replica_groups=mesh['shard'=2,'ctx'=4,'tp'=4] {'shard','ctx'}, dimensions={0}, use_global_device_ids=true | all-gather | bytes 10368 | tf_op jit(solution)/shard_map/all_gather | solution.py:137
  133.6 3.6 reduce-window.30
  140.0 34.6 %all_gather.44 = bf16[768,384]{1,0:T(8,128)(2,1)} all-gather(bf16[96,384]{1,0:T(8,128)(2,1)S(1)} %copy-done.49), channel_id=1, replica_groups=mesh['shard'=2,'ctx'=4,'tp'=4] {'shard','ctx'}, dimensions={0}, use_global_device_ids=true | all-gather | bytes 663552 | tf_op jit(solution)/shard_map/all_gather | solution.py:134
  174.6 34.8 %all_gather.45 = bf16[768,384]{1,0:T(8,128)(2,1)} all-gather(bf16[96,384]{1,0:T(8,128)(2,1)S(1)} %copy-done.50), channel_id=1, replica_groups=mesh['shard'=2,'ctx'=4,'tp'=4] {'shard','ctx'}, dimensions={0}, use_global_device_ids=true | all-gather | bytes 663552 | tf_op jit(solution)/shard_map/all_gather | solution.py:138
  209.5 7.8 %all-gather.1 = f32[4,1,6]{2,1,0:T(1,128)} all-gather(f32[1,1,6]{2,1,0:T(1,128)S(1)} %get-tuple-element.329), channel_id=1, replica_groups=mesh['shard'=2,'ctx'=4,'tp'=4] {'ctx'}, dimensions={0}, use_global_device_ids=true | all-gather | bytes 120 | tf_op jit(solution)/shard_map/all_gather | solution.py:20
  218.6 2.5 fusion.25
  223.2 1.6 reshape_reshape.6
  224.9 2.1 reshape.336
  226.9 1.8 copy.283
  228.7 1.8 copy.336
  230.5 1.8 fusion.49
  232.5 16.5 %all_gather.43 = f32[4,6,64,128]{3,2,1,0:T(8,128)} all-gather(f32[1,6,64,128]{3,2,1,0:T(8,128)S(1)} %slice_add_fusion.2), channel_id=1, replica_groups=mesh['shard'=2,'ctx'=4,'tp'=4] {'ctx'}, dimensions={0}, use_global_device_ids=true | all-gather | bytes 983040 | tf_op jit(solution)/shard_map/all_gather | solution.py:20
  249.5 1.8 reshape.335
  251.3 1.8 copy.282
  253.1 1.8 copy.337
  256.0 1.7 fusion.112
  258.5 4.0 fusion.35
  264.0 1.5 multiply_reduce_fusion.13
  265.5 5.6 psum.91
  271.1 3.6 multiply_reduce_fusion.8
  274.7 6.7 psum.93
  281.4 4.0 multiply_reduce_fusion.9
  285.4 2.6 reshape_reshape.7
  288.1 2.2 multiply_reduce_fusion.11
  290.3 6.0 fusion.9
  297.2 23.9 %all_gather.46 = f32[4,6,64,128]{3,2,1,0:T(8,128)} all-gather(f32[1,6,64,128]{3,2,1,0:T(8,128)S(1)} %slice_add_fusion.1), channel_id=1, replica_groups=mesh['shard'=2,'ctx'=4,'tp'=4] {'ctx'}, dimensions={0}, use_global_device_ids=true | all-gather | bytes 983040 | tf_op jit(solution)/shard_map/all_gather | solution.py:20
  321.2 5.4 while.27
  326.7 1.7 multiply_reduce_fusion.15
  328.4 2.9 multiply_reduce_fusion.10
  331.4 1.4 convolution_bitcast_fusion.2
  332.9 2.2 convolution_bitcast_fusion.1
  335.1 1.9 fusion.104
  338.9 15.8 %reduce-window.34 = f32[2,6,2,128]{3,2,1,0:T(2,128)S(1)} reduce-window(f32[2,6,2,128]{3,2,1,0:T(2,128)} %reshape.371, f32[]{:T(128)} %constant.100.clone.1), window={size=1x1x1x128 pad=0_0x0_0x0_0x0_127}, to_apply=%region_20.21 | reduce-window | flops 390144 | bytes 24580 | tf_op jit(solution)/shard_map/reduce-window.3
  365.3 15.1 %reduce-window.43 = f32[2,6,2,128]{3,2,1,0:T(2,128)S(1)} reduce-window(f32[2,6,2,128]{3,2,1,0:T(2,128)S(1)} %reshape.373, f32[]{:T(128)} %constant.100.clone.1), window={size=1x1x1x128 pad=0_0x0_0x0_0x0_127}, to_apply=%region_26.27 | reduce-window | flops 390144 | bytes 24580 | tf_op jit(solution)/shard_map/reduce-window.5
  381.4 4.2 fusion.32
  389.7 2.6 convolution_add_fusion
  392.2 1.8 copy.354
  394.0 1.9 pad_maximum_fusion.1
  396.3 1.8 fusion.113
  398.1 1.5 fusion.81
  401.4 1.6 fusion.88
  403.0 23.9 %all-reduce.17.cloned.1.call-done = f32[512,256]{0,1:T(8,128)} async-done(((f32[512,256]{0,1:T(8,128)}), f32[512,256]{0,1:T(8,128)}) %all-reduce.17.cloned.1.call-update) | async-done | bytes 524304 | tf_op jit(solution)/shard_map/psum | solution.py:265
  427.0 4.1 multiply_reduce_fusion.7
  434.4 7.6 %collective-permute-done.1 = f32[3,640]{0,1:T(8,128)S(1)} collective-permute-done((f32[3,640]{0,1:T(8,128)S(1)}, f32[3,640]{0,1:T(8,128)S(1)}, u32[]{:S(2)}, u32[]{:S(2)}) %collective-permute-start.1) | collective-permute-done | bytes 7712 | tf_op jit(solution)/shard_map/ppermute | solution.py:13
  444.3 1.8 add_add_fusion
  446.2 2.4 fusion.102
  448.7 1.6 convolution_bitcast_fusion
  450.3 3.0 copy.363
  453.4 1.7 fusion.114
  455.2 1.7 fusion.66
  457.8 4.8 reduce-scatter.16.cloned.1.call-done
  462.6 1.5 copy.362
  464.3 50.1 %all-reduce.19.cloned.1.call-done = (f32[512,768]{1,0:T(8,128)}, f32[512,768]{1,0:T(8,128)}) async-done(((f32[512,768]{1,0:T(8,128)}, f32[512,768]{1,0:T(8,128)}), (f32[512,768]{1,0:T(8,128)}, f32[512,768]{1,0:T(8,128)})) %all-reduce.19.cloned.1.call-update) | async-done | bytes 3145744 | tf_op jit(solution)/shard_map/psum | solution.py:215
  514.4 1.8 multiply_reduce_fusion.1
  516.2 37.9 %all-reduce.12 = (f32[768]{0:T(1024)S(1)}, f32[4,384]{1,0:T(4,128)}, f32[384]{0:T(512)}, f32[4,256]{1,0:T(4,128)}, f32[256]{0:T(256)}, /*index=5*/f32[6]{0:T(128)}, f32[6]{0:T(128)}, f32[6]{0:T(128)}, f32[384]{0:T(512)}) all-reduce(f32[768]{0:T(1024)S(1)} %get-tuple-element.246, ...), channel_id=2, replica_groups=mesh['shard'=2,'ctx'=4,'tp'=4] {'shard','ctx'}, use_global_device_ids=true, to_apply=%region_31.32.clone | all-reduce | flops 4370 | bytes 34960
  554.7 4.5 multiply_subtract_fusion
  559.3 37.2 %reduce-scatter.18.cloned.1.call-done = f32[96,384]{1,0:T(8,128)} async-done(((f32[768,384]{1,0:T(8,128)}), f32[96,384]{1,0:T(8,128)}) %reduce-scatter.18.cloned.1.call-update) | async-done | bytes 147472
  596.5 67.8 %reduce-scatter.10.cloned.1.call-done = f32[96,384]{1,0:T(8,128)} async-done(((f32[768,384]{1,0:T(8,128)}), f32[96,384]{1,0:T(8,128)}) %reduce-scatter.10.cloned.1.call-update) | async-done | bytes 147472 | tf_op jit(solution)/shard_map/reduce_scatter | solution.py:305
  664.3 67.8 %reduce-scatter.12.cloned.1.call-done = f32[96,384]{1,0:T(8,128)} async-done(((f32[768,384]{1,0:T(8,128)}), f32[96,384]{1,0:T(8,128)}) %reduce-scatter.12.cloned.1.call-update) | async-done | bytes 147472 | tf_op jit(solution)/shard_map/reduce_scatter | solution.py:306
  (376 shorter events, 49.5 us)
Async XLA Ops:
  8.0 93.0 %copy-start = (f32[512,768]{1,0:T(8,128)S(1)}, f32[512,768]{1,0:T(8,128)}, u32[]{:S(2)}) copy-start(f32[512,768]{1,0:T(8,128)} %param.22) | copy-start | bytes 4718596
  8.0 61.5 %copy-start.60 = (bf16[96,256]{1,0:T(8,128)(2,1)S(1)}, bf16[96,256]{1,0:T(8,128)(2,1)}, u32[]{:S(2)}) copy-start(bf16[96,256]{1,0:T(8,128)(2,1)} %param.26) | copy-start | bytes 147460
  8.0 418.9 %all-reduce.17.cloned.1.call-start = ((), (), s32[]{:S(2)}) async-start(), calls=%async_computation.5 | async-start | bytes 1048576 | tf_op jit(solution)/shard_map/psum | solution.py:265
  34.3 66.9 %copy-start.51 = (f32[768]{0:T(1024)}, f32[768]{0:T(1024)S(1)}, u32[]{:S(2)}) copy-start(f32[768]{0:T(1024)S(1)} %convert_element_type.71) | copy-start | bytes 9220
  36.5 64.7 %copy-start.78 = (f32[512]{0:T(512)}, f32[512]{0:T(512)S(1)}, u32[]{:S(2)}) copy-start(f32[512]{0:T(512)S(1)} %get-tuple-element.322) | copy-start | bytes 6148
  69.5 32.2 %copy-start.28 = (bf16[768,384]{1,0:T(8,128)(2,1)}, bf16[768,384]{1,0:T(8,128)(2,1)S(1)}, u32[]{:S(2)}) copy-start(bf16[768,384]{1,0:T(8,128)(2,1)S(1)} %all_gather.19) | copy-start | bytes 1769476
  101.8 30.7 %copy-start.110 = (s32[512]{0:T(512)S(1)}, s32[512]{0:T(512)}, u32[]{:S(2)}) copy-start(s32[512]{0:T(512)} %param.38) | copy-start | bytes 6148
  101.8 30.7 %copy-start.117 = (f32[6]{0:T(128)S(1)}, f32[6]{0:T(128)}, u32[]{:S(2)}) copy-start(f32[6]{0:T(128)} %param.34) | copy-start | bytes 76
  101.8 30.7 %copy-start.119 = (f32[6]{0:T(128)S(1)}, f32[6]{0:T(128)}, u32[]{:S(2)}) copy-start(f32[6]{0:T(128)} %param.33) | copy-start | bytes 76
  101.8 37.2 %copy-start.100 = (f32[4,384]{1,0:T(4,128)S(1)}, f32[4,384]{1,0:T(4,128)}, u32[]{:S(2)}) copy-start(f32[4,384]{1,0:T(4,128)} %param.29) | copy-start | bytes 18436
  101.8 37.2 %copy-start.103 = (f32[4,256]{1,0:T(4,128)S(1)}, f32[4,256]{1,0:T(4,128)}, u32[]{:S(2)}) copy-start(f32[4,256]{1,0:T(4,128)} %param.31) | copy-start | bytes 12292
  101.8 38.1 %copy-start.49 = (bf16[96,384]{1,0:T(8,128)(2,1)S(1)}, bf16[96,384]{1,0:T(8,128)(2,1)}, u32[]{:S(2)}) copy-start(bf16[96,384]{1,0:T(8,128)(2,1)} %param.24) | copy-start | bytes 221188
  102.3 72.3 %copy-start.50 = (bf16[96,384]{1,0:T(8,128)(2,1)S(1)}, bf16[96,384]{1,0:T(8,128)(2,1)}, u32[]{:S(2)}) copy-start(bf16[96,384]{1,0:T(8,128)(2,1)} %param.28) | copy-start | bytes 221188
  102.4 107.1 %copy-start.108 = (f32[384]{0:T(512)S(1)}, f32[384]{0:T(512)}, u32[]{:S(2)}) copy-start(f32[384]{0:T(512)} %param.30) | copy-start | bytes 4612
  102.4 107.1 %copy-start.115 = (f32[256]{0:T(256)S(1)}, f32[256]{0:T(256)}, u32[]{:S(2)}) copy-start(f32[256]{0:T(256)} %param.32) | copy-start | bytes 3076
  102.4 115.0 %copy-start.116 = (f32[6]{0:T(128)S(1)}, f32[6]{0:T(128)}, u32[]{:S(2)}) copy-start(f32[6]{0:T(128)} %param.35) | copy-start | bytes 76
  102.5 115.7 %collective-permute-start = (bf16[3,640]{0,1:T(8,128)(2,1)S(1)}, bf16[3,640]{0,1:T(8,128)(2,1)S(1)}, u32[]{:S(2)}, u32[]{:S(2)}) collective-permute-start(bf16[3,640]{0,1:T(8,128)(2,1)S(1)} %pad_maximum_fusion.8), channel_id=1, source_target_pairs={{0,4},{4,8},{8,12},{1,5},{5,9},{9,13},{2,6},{6,10},{10,14},{3,7},{... | collective-permute-start | bytes 11528 | tf_op jit(solution)/shard_map/ppermute | solution.py:13
  105.3 112.8 %copy-start.84 = (f32[2,256]{1,0:T(2,128)}, f32[2,256]{1,0:T(2,128)S(1)}, u32[]{:S(2)}) copy-start(f32[2,256]{1,0:T(2,128)S(1)} %get-tuple-element.323) | copy-start | bytes 6148
  105.3 112.8 %copy-start.93 = (pred[2,256]{1,0:T(4,128)(4,1)}, pred[2,256]{1,0:T(4,128)(4,1)S(1)}, u32[]{:S(2)}) copy-start(pred[2,256]{1,0:T(4,128)(4,1)S(1)} %get-tuple-element.324) | copy-start | bytes 1540
  105.3 33.7 %copy-start.104 = (f32[2]{0:T(128)}, f32[2]{0:T(128)S(1)}, u32[]{:S(2)}) copy-start(f32[2]{0:T(128)S(1)} %compare_convert_fusion.1) | copy-start | bytes 28
  132.5 6.0 copy-start.47
  133.5 247.9 %copy-start.41 = (f32[512,6]{0,1:T(8,128)}, f32[512,6]{0,1:T(8,128)S(1)}, u32[]{:S(2)}) copy-start(f32[512,6]{0,1:T(8,128)S(1)} %get-tuple-element.332) | copy-start | bytes 36868
  137.8 80.3 %copy-start.80 = (f32[2,6]{1,0:T(2,128)}, f32[2,6]{1,0:T(2,128)S(1)}, u32[]{:S(2)}) copy-start(f32[2,6]{1,0:T(2,128)S(1)} %slice_reduce_fusion) | copy-start | bytes 148
  139.1 79.4 %copy-start.61 = (f32[640]{0:T(1024)}, f32[640]{0:T(1024)S(1)}, u32[]{:S(2)}) copy-start(f32[640]{0:T(1024)S(1)} %get-tuple-element.259) | copy-start | bytes 7684
  139.1 79.4 %copy-start.63 = (f32[640]{0:T(1024)}, f32[640]{0:T(1024)S(1)}, u32[]{:S(2)}) copy-start(f32[640]{0:T(1024)S(1)} %get-tuple-element.260) | copy-start | bytes 7684
  139.1 79.4 %copy-start.65 = (f32[640]{0:T(1024)}, f32[640]{0:T(1024)S(1)}, u32[]{:S(2)}) copy-start(f32[640]{0:T(1024)S(1)} %get-tuple-element.261) | copy-start | bytes 7684
  139.1 79.4 %copy-start.67 = (f32[640]{0:T(1024)}, f32[640]{0:T(1024)S(1)}, u32[]{:S(2)}) copy-start(f32[640]{0:T(1024)S(1)} %get-tuple-element.262) | copy-start | bytes 7684
  174.6 43.9 %copy-start.72 = (f32[512]{0:T(512)S(1)}, f32[512]{0:T(512)}, u32[]{:S(2)}) copy-start(f32[512]{0:T(512)} %get-tuple-element.318) | copy-start | bytes 6148
  174.6 43.9 %copy-start.74 = (f32[512]{0:T(512)S(1)}, f32[512]{0:T(512)}, u32[]{:S(2)}) copy-start(f32[512]{0:T(512)} %get-tuple-element.319) | copy-start | bytes 6148
  174.6 43.9 %copy-start.76 = (f32[512]{0:T(512)S(1)}, f32[512]{0:T(512)}, u32[]{:S(2)}) copy-start(f32[512]{0:T(512)} %get-tuple-element.320) | copy-start | bytes 6148
  224.9 33.6 %copy-start.6 = (f32[2,256,6,64]{1,0,3,2:T(2,128)}, f32[2,256,6,64]{1,0,3,2:T(2,128)S(1)}, u32[]{:S(2)}) copy-start(f32[2,256,6,64]{1,0,3,2:T(2,128)S(1)} %reshape_reshape.6) | copy-start | bytes 2359300
  224.9 7.5 %copy-start.101 = (f32[6]{0:T(128)S(1)}, f32[6]{0:T(128)}, u32[]{:S(2)}) copy-start(f32[6]{0:T(128)} %get-tuple-element.328) | copy-start | bytes 76
  224.9 7.5 %copy-start.106 = (f32[6]{0:T(128)S(1)}, f32[6]{0:T(128)}, u32[]{:S(2)}) copy-start(f32[6]{0:T(128)} %get-tuple-element.326) | copy-start | bytes 76
  232.3 16.6 %copy-start.21 = (f32[2,6,64,128]{3,2,1,0:T(8,128)}, f32[2,6,64,128]{3,2,1,0:T(8,128)S(1)}, u32[]{:S(2)}) copy-start(f32[2,6,64,128]{3,2,1,0:T(8,128)S(1)} %fusion.49) | copy-start | bytes 1179652
  264.0 7.1 copy-start.69
  265.5 15.9 %copy-start.3 = (f32[512,384]{0,1:T(8,128)}, f32[512,384]{0,1:T(8,128)S(1)}, u32[]{:S(2)}) copy-start(f32[512,384]{0,1:T(8,128)S(1)} %get-tuple-element.302) | copy-start | bytes 2359300
  271.1 10.3 %copy-start.57 = (f32[512]{0:T(512)}, f32[512]{0:T(512)S(1)}, u32[]{:S(2)}) copy-start(f32[512]{0:T(512)S(1)} %add_rsqrt_fusion) | copy-start | bytes 6148
  290.3 6.8 copy-start.105
  297.1 24.1 %copy-start.27 = (f32[2,6,64,128]{3,2,1,0:T(8,128)}, f32[2,6,64,128]{3,2,1,0:T(8,128)S(1)}, u32[]{:S(2)}) copy-start(f32[2,6,64,128]{3,2,1,0:T(8,128)S(1)} %fusion.46) | copy-start | bytes 1179652
  297.2 29.4 %copy-start.99 = (f32[6]{0:T(128)S(1)}, f32[6]{0:T(128)}, u32[]{:S(2)}) copy-start(f32[6]{0:T(128)} %get-tuple-element.327) | copy-start | bytes 76
  297.2 29.4 %copy-start.102 = (f32[6]{0:T(128)S(1)}, f32[6]{0:T(128)}, u32[]{:S(2)}) copy-start(f32[6]{0:T(128)} %get-tuple-element.328) | copy-start | bytes 76
  321.2 7.2 copy-start.33
  331.4 29.4 %copy-start.43 = (f32[2,256,6]{1,2,0:T(8,128)}, f32[2,256,6]{1,2,0:T(8,128)S(1)}, u32[]{:S(2)}) copy-start(f32[2,256,6]{1,2,0:T(8,128)S(1)} %get-tuple-element.336) | copy-start | bytes 36868
  335.1 46.3 %copy-start.11 = (f32[2,256,6,64]{1,0,3,2:T(2,128)S(1)}, f32[2,256,6,64]{1,0,3,2:T(2,128)}, u32[]{:S(2)}) copy-start(f32[2,256,6,64]{1,0,3,2:T(2,128)} %reshape_reshape.7) | copy-start | bytes 2359300
  389.7 6.6 copy-start.20
  389.7 6.6 copy-start.31
  396.0 66.7 %reduce-scatter.16.cloned.1.call-start = ((), (), s32[]{:S(2)}) async-start(), calls=%async_computation.9 | async-start | bytes 442368
  400.2 26.7 %copy-start.73 = (f32[512]{0:T(512)S(1)}, f32[512]{0:T(512)}, u32[]{:S(2)}) copy-start(f32[512]{0:T(512)} %get-tuple-element.318) | copy-start | bytes 6148
  400.2 26.7 %copy-start.75 = (f32[512]{0:T(512)S(1)}, f32[512]{0:T(512)}, u32[]{:S(2)}) copy-start(f32[512]{0:T(512)} %get-tuple-element.319) | copy-start | bytes 6148
  400.2 26.7 %copy-start.77 = (f32[512]{0:T(512)S(1)}, f32[512]{0:T(512)}, u32[]{:S(2)}) copy-start(f32[512]{0:T(512)} %get-tuple-element.320) | copy-start | bytes 6148
  403.0 111.4 %all-reduce.19.cloned.1.call-start = ((), (), s32[]{:S(2)}) async-start(), calls=%async_computation.11 | async-start | bytes 6291456 | tf_op jit(solution)/shard_map/psum | solution.py:215
  431.8 10.2 %collective-permute-start.1 = (f32[3,640]{0,1:T(8,128)S(1)}, f32[3,640]{0,1:T(8,128)S(1)}, u32[]{:S(2)}, u32[]{:S(2)}) collective-permute-start(f32[3,640]{0,1:T(8,128)S(1)} %pad_add_fusion.1), channel_id=1, source_target_pairs={{4,0},{8,4},{12,8},{5,1},{9,5},{13,9},{6,2},{10,6},{14,10},{7,3},{... | collective-permute-start | bytes 23048 | tf_op jit(solution)/shard_map/ppermute | solution.py:13
  434.4 8.1 %copy-start.26 = (bf16[768,256]{1,0:T(8,128)(2,1)S(1)}, bf16[768,256]{1,0:T(8,128)(2,1)}, u32[]{:S(2)}) copy-start(bf16[768,256]{1,0:T(8,128)(2,1)} %copy-done.25) | copy-start | bytes 1179652
  446.1 113.1 %reduce-scatter.14.cloned.1.call-start = ((), (), s32[]{:S(2)}) async-start(), calls=%async_computation.8 | async-start | bytes 884736 | tf_op jit(solution)/shard_map/reduce_scatter | solution.py:307
  448.6 147.9 %reduce-scatter.18.cloned.1.call-start = ((), (), s32[]{:S(2)}) async-start(), calls=%async_computation.10 | async-start | bytes 1327104
  453.3 211.0 %reduce-scatter.10.cloned.1.call-start = ((), (), s32[]{:S(2)}) async-start(), calls=%async_computation.6 | async-start | bytes 1327104 | tf_op jit(solution)/shard_map/reduce_scatter | solution.py:305
  455.1 9.0 %copy-start.90 = (f32[640]{0:T(1024)S(1)}, f32[640]{0:T(1024)}, u32[]{:S(2)}) copy-start(f32[640]{0:T(1024)} %get-tuple-element.248) | copy-start | bytes 7684
  455.1 9.0 %copy-start.89 = (f32[640]{0:T(1024)S(1)}, f32[640]{0:T(1024)}, u32[]{:S(2)}) copy-start(f32[640]{0:T(1024)} %get-tuple-element.249) | copy-start | bytes 7684
  455.1 9.0 %copy-start.88 = (f32[640]{0:T(1024)S(1)}, f32[640]{0:T(1024)}, u32[]{:S(2)}) copy-start(f32[640]{0:T(1024)} %get-tuple-element.250) | copy-start | bytes 7684
  455.1 59.2 %copy-start.1 = (f32[512,768]{1,0:T(8,128)S(1)}, f32[512,768]{1,0:T(8,128)}, u32[]{:S(2)}) copy-start(f32[512,768]{1,0:T(8,128)} %param.22) | copy-start | bytes 4718596
  455.2 59.2 %copy-start.52 = (f32[768]{0:T(1024)S(1)}, f32[768]{0:T(1024)}, u32[]{:S(2)}) copy-start(f32[768]{0:T(1024)} %copy-done.51) | copy-start | bytes 9220
  455.2 59.2 %copy-start.79 = (f32[512]{0:T(512)S(1)}, f32[512]{0:T(512)}, u32[]{:S(2)}) copy-start(f32[512]{0:T(512)} %copy-done.78) | copy-start | bytes 6148
  455.2 277.0 %reduce-scatter.12.cloned.1.call-start = ((), (), s32[]{:S(2)}) async-start(), calls=%async_computation.7 | async-start | bytes 1327104 | tf_op jit(solution)/shard_map/reduce_scatter | solution.py:306
  514.4 40.4 %copy-start.96 = (f32[512]{0:T(512)S(1)}, f32[512]{0:T(512)}, u32[]{:S(2)}) copy-start(f32[512]{0:T(512)} %get-tuple-element.321) | copy-start | bytes 6148
  (66 other events, 183.7 us)
Sparse Core Ops, SparseCore 0:
  396.1 30.8 all-reduce.16
  446.2 68.0 all-reduce.18
Sparse Core Ops, SparseCore 1:
  403.0 59.5 reduce-scatter.15
  466.4 62.3 reduce-scatter.13
  532.6 63.8 reduce-scatter.17
  600.5 63.8 reduce-scatter.9
  668.3 63.8 reduce-scatter.11
where the time goes:
time: 747 us; the launch traced here: 740 us
  blocking collectives  283 us (38%)
  waiting for transfers between devices  259 us (35%)
  other arithmetic  79.2 us (11%)
  matrix products  52.3 us (7%)
  local copies, waits for them, and re-layouts  43.6 us (6%)
  between operations  18.8 us (3%)
    reduce_scatter x1, waiting for transfers between devices, local(): lax.psum_scatter(d_w_x, ('shard', 'ctx'), scatter_dimension=0, tiled=True)  67.8 us
    reduce_scatter x1, waiting for transfers between devices, local(): lax.psum_scatter(d_w_z, ('shard', 'ctx'), scatter_dimension=0, tiled=True)  67.8 us
    unnamed x2, blocking collectives  61.2 us
    psum x1, waiting for transfers between devices, local(): block_out = x_in + lax.psum(contract_cols(mixed, wout_all), 'tp')  50.1 us
    all_gather x3, blocking collectives, entering_2(): gathered = jax.tree.map(lambda a: lax.all_gather(a, axis), part)  48.2 us
    unnamed x9, waiting for transfers between devices  42.1 us
    another operation x12, other arithmetic  38.2 us
    all_gather x1, blocking collectives, local(): lax.all_gather(w_out, ('shard', 'ctx'), axis=0, tiled=True)  34.8 us
  transfers between devices with their start and end apart: 9, of which 7 were waited for; matrix products, arithmetic and copies ran while one was open for 6% of the time, Pallas kernels for 0%

commit v1 on v0

--- a/solution.py
+++ b/solution.py
@@ -212,7 +212,7 @@
     square_sum = lax.psum(jnp.sum(gated * gated, axis=1), "tp")
     inv_gate = lax.rsqrt(square_sum / inner_total + norm_eps)
     mixed = (gated * inv_gate[:, None] * gate_gain[None, :]).astype(jnp.bfloat16)
-    block_out = x_in + lax.psum(contract_cols(mixed, wout_all), "tp")
+    block_out = x_in + jnp.sum(lax.all_gather(contract_cols(mixed, wout_all), "tp"), axis=0)
     weights_back = (
         lax.all_gather(norm_gain, ("shard", "ctx"), axis=0, tiled=True),
         lax.all_gather(w_z, ("shard", "ctx"), axis=0, tiled=True),

time: 747 us -> 722 us (0.967)
  local copies, waits for them, and re-layouts: 43.6 us -> 26.7 us
    unnamed x9 -> x10, waiting for transfers between devices: 42.1 us -> 95.1 us
    psum x1, waiting for transfers between devices: 50.1 us -> 0.02 us  [local(): d_normed = lax.psum(d_normed_part, 'tp')]
    psum x1, waiting for transfers between devices: 23.9 us -> 0.02 us  [local(): lax.psum(jnp.concatenate([(g_b + s_b).reshape(row_count, state_width), g_...]
    reduce_scatter x1, waiting for transfers between devices: 0.01 us -> 8.76 us  [local(): lax.psum_scatter(d_w_bc, ('shard', 'ctx'), scatter_dimension=0, tiled=True)]
    all_gather x0 -> x1, waiting for transfers between devices: none -> 8.21 us  [local(): lax.all_gather(contract_cols(mixed, wout_all), 'tp')]
  transfers between devices with their start and end apart: 9 -> 10, of which waited for: 7 -> 7; matrix products, arithmetic and copies ran while one was open for 6% -> 12% of each run, Pallas kernels for 0% -> 0%
where the time goes in v1:
time: 722 us; the launch traced here: 715 us
  blocking collectives  279 us (39%)
  waiting for transfers between devices  254 us (35%)
  other arithmetic  77.3 us (11%)
  matrix products  55.1 us (8%)
  local copies, waits for them, and re-layouts  26.7 us (4%)
  between operations  18.6 us (3%)
    unnamed x10, waiting for transfers between devices  95.1 us
    reduce_scatter x1, waiting for transfers between devices, local(): lax.psum_scatter(d_w_x, ('shard', 'ctx'), scatter_dimension=0, tiled=True)  67.7 us
    reduce_scatter x1, waiting for transfers between devices, local(): lax.psum_scatter(d_w_z, ('shard', 'ctx'), scatter_dimension=0, tiled=True)  67.6 us
    unnamed x2, blocking collectives  57.6 us
    all_gather x3, blocking collectives, entering_2(): gathered = jax.tree.map(lambda a: lax.all_gather(a, axis), part)  45.6 us
    all_gather x1, blocking collectives, local(): lax.all_gather(w_z, ('shard', 'ctx'), axis=0, tiled=True)  34.9 us
    another operation x12, other arithmetic  34.9 us
    all_gather x1, blocking collectives, local(): lax.all_gather(w_out, ('shard', 'ctx'), axis=0, tiled=True)  34.7 us
  transfers between devices with their start and end apart: 10, of which 7 were waited for; matrix products, arithmetic and copies ran while one was open for 12% of the time, Pallas kernels for 0%

profile of v1, /device:TPU:0, one launch (start us, length us, event | category | flops | bytes accessed | tf_op | source)
XLA Modules:
  0.0 714.8 jit_solution(2781560469763815800)
XLA Ops:
  8.1 34.0 %all_gather.46 = bf16[768,256]{1,0:T(8,128)(2,1)S(1)} all-gather(bf16[96,256]{1,0:T(8,128)(2,1)} %param.26), channel_id=1, replica_groups=mesh['shard'=2,'ctx'=4,'tp'=4] {'shard','ctx'}, dimensions={0}, use_global_device_ids=true | all-gather | bytes 442368 | tf_op jit(solution)/shard_map/all_gather | solution.py:136
  42.0 1.3 fusion.111
  44.9 21.6 %all-reduce.10 = bf16[768]{0:T(1024)(128)(2,1)S(1)} all-reduce(bf16[768]{0:T(1024)(128)(2,1)S(1)} %dynamic-update-slice), channel_id=1, replica_groups=mesh['shard'=2,'ctx'=4,'tp'=4] {'shard','ctx'}, use_global_device_ids=true, to_apply=%add.10 | all-reduce | flops 768 | bytes 3072
  66.5 1.6 multiply_reduce_fusion.3
  68.7 32.2 %all_gather.45 = bf16[768,384]{1,0:T(8,128)(2,1)S(1)} all-gather(bf16[96,384]{1,0:T(8,128)(2,1)S(1)} %copy-done.47), channel_id=1, replica_groups=mesh['shard'=2,'ctx'=4,'tp'=4] {'shard','ctx'}, dimensions={0}, use_global_device_ids=true | all-gather | bytes 663552 | tf_op jit(solution)/shard_map/all_gather | solution.py:135
  102.5 1.4 collective-permute-start
  105.4 27.1 %all-gather.1 = bf16[8,96,6]{1,2,0:T(8,128)(2,1)S(1)} all-gather(bf16[1,96,6]{1,2,0:T(8,128)(2,1)S(1)} %bitcast.234), channel_id=1, replica_groups=mesh['shard'=2,'ctx'=4,'tp'=4] {'shard','ctx'}, dimensions={0}, use_global_device_ids=true | all-gather | bytes 10368 | tf_op jit(solution)/shard_map/all_gather | solution.py:137
  133.6 3.6 reduce-window.30
  139.9 34.9 %all_gather.50 = bf16[768,384]{1,0:T(8,128)(2,1)} all-gather(bf16[96,384]{1,0:T(8,128)(2,1)S(1)} %copy-done.48), channel_id=1, replica_groups=mesh['shard'=2,'ctx'=4,'tp'=4] {'shard','ctx'}, dimensions={0}, use_global_device_ids=true | all-gather | bytes 663552 | tf_op jit(solution)/shard_map/all_gather | solution.py:134
  174.8 34.7 %all_gather.51 = bf16[768,384]{1,0:T(8,128)(2,1)} all-gather(bf16[96,384]{1,0:T(8,128)(2,1)S(1)} %copy-done.49), channel_id=1, replica_groups=mesh['shard'=2,'ctx'=4,'tp'=4] {'shard','ctx'}, dimensions={0}, use_global_device_ids=true | all-gather | bytes 663552 | tf_op jit(solution)/shard_map/all_gather | solution.py:138
  209.6 8.1 %all-gather.2 = f32[4,1,6]{2,1,0:T(1,128)S(1)} all-gather(f32[1,1,6]{2,1,0:T(1,128)S(1)} %get-tuple-element.327), channel_id=1, replica_groups=mesh['shard'=2,'ctx'=4,'tp'=4] {'ctx'}, dimensions={0}, use_global_device_ids=true | all-gather | bytes 120 | tf_op jit(solution)/shard_map/all_gather | solution.py:20
  218.3 2.5 fusion.25
  226.6 1.6 reshape_reshape.6
  228.2 2.0 fusion.49
  230.4 16.4 %all_gather.49 = f32[4,6,64,128]{3,2,1,0:T(8,128)} all-gather(f32[1,6,64,128]{3,2,1,0:T(8,128)S(1)} %slice_add_fusion.2), channel_id=1, replica_groups=mesh['shard'=2,'ctx'=4,'tp'=4] {'ctx'}, dimensions={0}, use_global_device_ids=true | all-gather | bytes 983040 | tf_op jit(solution)/shard_map/all_gather | solution.py:20
  247.1 1.7 fusion.112
  248.8 1.2 fusion.76
  250.9 4.0 fusion.35
  256.4 1.5 multiply_reduce_fusion.13
  257.8 5.6 psum.84
  263.5 3.5 multiply_reduce_fusion.8
  267.0 7.2 %psum.85 = f32[512]{0:T(512)S(1)} all-reduce(f32[512]{0:T(512)S(1)} %get-tuple-element.253), channel_id=1, replica_groups=mesh['shard'=2,'ctx'=4,'tp'=4] {'tp'}, use_global_device_ids=true, to_apply=%region_11.12 | all-reduce | flops 512 | bytes 4096 | tf_op jit(solution)/shard_map/psum | solution.py:229
  274.2 4.0 multiply_reduce_fusion.9
  278.3 2.6 reshape_reshape.7
  280.8 3.3 convolution_bitcast_fusion.1
  284.2 7.4 %fusion.9 = (f32[2,256,6]{1,2,0:T(8,128)}, f32[2,256,6]{1,2,0:T(8,128)}, f32[2,256,6]{1,2,0:T(8,128)}, f32[2,256,256]{2,1,0:T(8,128)}) fusion(f32[2,256,6]{1,2,0:T(8,128)S(1)} %bitcast.221, f32[2,256,6]{1,2,0:T(8,128)S(1)} %bitcast.215, f32[2,256,256]{2,1,0:T(8,128)} %copy-done.40, pred[2,256,256]{2,1,0:T(8,128)(4,1)} %compare_and_fusion, ...), kind=kOutput, calls=%fused_computation.17 | convolution fusion | flops 615635968 | bytes 2813952 | tf_op jit(solution)/shard_map/transpose(jvp(vmap(tsh,shp->thp)))/dot_general | solution.py:65
  292.5 21.1 %all_gather.54 = f32[4,6,64,128]{3,2,1,0:T(8,128)} all-gather(f32[1,6,64,128]{3,2,1,0:T(8,128)S(1)} %slice_add_fusion.1), channel_id=1, replica_groups=mesh['shard'=2,'ctx'=4,'tp'=4] {'ctx'}, dimensions={0}, use_global_device_ids=true | all-gather | bytes 983040 | tf_op jit(solution)/shard_map/all_gather | solution.py:20
  313.6 3.4 while.27
  313.7 1.1 bitcast_add_fusion.9
  317.1 1.8 multiply_reduce_fusion.15
  318.8 3.4 convolution_bitcast_fusion.2
  322.3 2.3 multiply_reduce_fusion.10
  326.8 3.0 convolution_add_fusion.1
  329.7 1.1 copy.353
  330.8 1.8 pad_maximum_fusion.1
  332.7 4.2 fusion.32
  339.9 15.1 %reduce-window.43 = f32[2,6,2,128]{3,2,1,0:T(2,128)S(1)} reduce-window(f32[2,6,2,128]{3,2,1,0:T(2,128)S(1)} %reshape.374, f32[]{:T(128)} %constant.100.clone.1), window={size=1x1x1x128 pad=0_0x0_0x0_0x0_127}, to_apply=%region_26.27 | reduce-window | flops 390144 | bytes 24580 | tf_op jit(solution)/shard_map/reduce-window.5
  356.2 15.1 %reduce-window.34 = f32[2,6,2,128]{3,2,1,0:T(2,128)S(1)} reduce-window(f32[2,6,2,128]{3,2,1,0:T(2,128)S(1)} %reshape.372, f32[]{:T(128)} %constant.100.clone.1), window={size=1x1x1x128 pad=0_0x0_0x0_0x0_127}, to_apply=%region_20.21 | reduce-window | flops 390144 | bytes 24580 | tf_op jit(solution)/shard_map/reduce-window.3
  371.7 1.8 fusion.113
  373.4 1.5 fusion.81
  375.6 1.2 fusion.86
  376.7 1.6 fusion.88
  378.7 4.0 multiply_reduce_fusion.7
  383.4 1.3 collective-permute-start.1
  384.7 1.3 pad_add_fusion
  386.1 7.0 collective-permute-done.1
  395.4 1.8 add_add_fusion
  398.5 1.8 fusion.104
  400.5 1.3 fusion.102
  401.8 1.7 fusion.114
  403.7 1.5 convolution_bitcast_fusion
  405.2 2.7 copy.363
  408.1 1.6 fusion.66
  410.7 27.3 %reduce-scatter.16.cloned.1.call-done = f32[96,6]{1,0:T(8,128)} async-done(((f32[768,6]{1,0:T(8,128)}), f32[96,6]{1,0:T(8,128)}) %reduce-scatter.16.cloned.1.call-update) | async-done | bytes 2320
  438.0 1.5 copy.362
  439.7 1.8 multiply_reduce_fusion.1
  441.6 36.0 %all-reduce.12 = (f32[768]{0:T(1024)S(1)}, f32[4,384]{1,0:T(4,128)}, f32[384]{0:T(512)}, f32[4,256]{1,0:T(4,128)}, f32[256]{0:T(256)}, /*index=5*/f32[6]{0:T(128)}, f32[6]{0:T(128)}, f32[6]{0:T(128)}, f32[384]{0:T(512)}) all-reduce(f32[768]{0:T(1024)S(1)} %get-tuple-element.246, ...), channel_id=3, replica_groups=mesh['shard'=2,'ctx'=4,'tp'=4] {'shard','ctx'}, use_global_device_ids=true, to_apply=%region_31.32.clone | all-reduce | flops 4370 | bytes 34960
  478.2 8.2 %all-gather.5.cloned.1.call-done = f32[2048,768]{1,0:T(8,128)} async-done(((f32[512,768]{1,0:T(8,128)}), f32[2048,768]{1,0:T(8,128)}) %all-gather.5.cloned.1.call-update) | async-done | bytes 6291472 | tf_op jit(solution)/shard_map/all_gather | solution.py:215
  486.4 4.5 reduce_sum.247
  490.9 4.5 multiply_subtract_fusion
  495.5 8.8 %reduce-scatter.14.cloned.1.call-done = f32[96,256]{1,0:T(8,128)} async-done(((f32[768,256]{1,0:T(8,128)}), f32[96,256]{1,0:T(8,128)}) %reduce-scatter.14.cloned.1.call-update) | async-done | bytes 98320 | tf_op jit(solution)/shard_map/reduce_scatter | solution.py:307
  504.2 67.6 %reduce-scatter.10.cloned.1.call-done = f32[96,384]{1,0:T(8,128)} async-done(((f32[768,384]{1,0:T(8,128)}), f32[96,384]{1,0:T(8,128)}) %reduce-scatter.10.cloned.1.call-update) | async-done | bytes 147472 | tf_op jit(solution)/shard_map/reduce_scatter | solution.py:305
  571.8 67.7 %reduce-scatter.18.cloned.1.call-done = f32[96,384]{1,0:T(8,128)} async-done(((f32[768,384]{1,0:T(8,128)}), f32[96,384]{1,0:T(8,128)}) %reduce-scatter.18.cloned.1.call-update) | async-done | bytes 147472
  639.5 67.7 %reduce-scatter.12.cloned.1.call-done = f32[96,384]{1,0:T(8,128)} async-done(((f32[768,384]{1,0:T(8,128)}), f32[96,384]{1,0:T(8,128)}) %reduce-scatter.12.cloned.1.call-update) | async-done | bytes 147472 | tf_op jit(solution)/shard_map/reduce_scatter | solution.py:306
  (364 shorter events, 33.3 us)
Async XLA Ops:
  8.0 92.8 %copy-start = (f32[512,768]{1,0:T(8,128)S(1)}, f32[512,768]{1,0:T(8,128)}, u32[]{:S(2)}) copy-start(f32[512,768]{1,0:T(8,128)} %param.22) | copy-start | bytes 4718596
  8.0 60.6 %copy-start.47 = (bf16[96,384]{1,0:T(8,128)(2,1)S(1)}, bf16[96,384]{1,0:T(8,128)(2,1)}, u32[]{:S(2)}) copy-start(bf16[96,384]{1,0:T(8,128)(2,1)} %param.25) | copy-start | bytes 221188
  8.0 370.6 %all-reduce.16.cloned.1.call-start = ((), (), s32[]{:S(2)}) async-start(), calls=%async_computation.5 | async-start | bytes 1048576 | tf_op jit(solution)/shard_map/psum | solution.py:265
  42.0 59.0 %copy-start.25 = (bf16[768,256]{1,0:T(8,128)(2,1)}, bf16[768,256]{1,0:T(8,128)(2,1)S(1)}, u32[]{:S(2)}) copy-start(bf16[768,256]{1,0:T(8,128)(2,1)S(1)} %all_gather.46) | copy-start | bytes 1179652
  66.5 34.6 %copy-start.50 = (f32[768]{0:T(1024)}, f32[768]{0:T(1024)S(1)}, u32[]{:S(2)}) copy-start(f32[768]{0:T(1024)S(1)} %convert_element_type.71) | copy-start | bytes 9220
  68.7 32.8 %copy-start.72 = (f32[512]{0:T(512)}, f32[512]{0:T(512)S(1)}, u32[]{:S(2)}) copy-start(f32[512]{0:T(512)S(1)} %get-tuple-element.320) | copy-start | bytes 6148
  101.7 30.9 %copy-start.109 = (f32[6]{0:T(128)S(1)}, f32[6]{0:T(128)}, u32[]{:S(2)}) copy-start(f32[6]{0:T(128)} %param.34) | copy-start | bytes 76
  101.7 30.9 %copy-start.111 = (f32[6]{0:T(128)S(1)}, f32[6]{0:T(128)}, u32[]{:S(2)}) copy-start(f32[6]{0:T(128)} %param.33) | copy-start | bytes 76
  101.7 37.2 %copy-start.91 = (f32[4,384]{1,0:T(4,128)S(1)}, f32[4,384]{1,0:T(4,128)}, u32[]{:S(2)}) copy-start(f32[4,384]{1,0:T(4,128)} %param.29) | copy-start | bytes 18436
  101.7 37.2 %copy-start.93 = (f32[4,256]{1,0:T(4,128)S(1)}, f32[4,256]{1,0:T(4,128)}, u32[]{:S(2)}) copy-start(f32[4,256]{1,0:T(4,128)} %param.31) | copy-start | bytes 12292
  102.3 37.6 %copy-start.48 = (bf16[96,384]{1,0:T(8,128)(2,1)S(1)}, bf16[96,384]{1,0:T(8,128)(2,1)}, u32[]{:S(2)}) copy-start(bf16[96,384]{1,0:T(8,128)(2,1)} %param.24) | copy-start | bytes 221188
  102.3 72.5 %copy-start.49 = (bf16[96,384]{1,0:T(8,128)(2,1)S(1)}, bf16[96,384]{1,0:T(8,128)(2,1)}, u32[]{:S(2)}) copy-start(bf16[96,384]{1,0:T(8,128)(2,1)} %param.28) | copy-start | bytes 221188
  102.4 107.2 %copy-start.101 = (f32[384]{0:T(512)S(1)}, f32[384]{0:T(512)}, u32[]{:S(2)}) copy-start(f32[384]{0:T(512)} %param.30) | copy-start | bytes 4612
  102.4 107.2 %copy-start.107 = (f32[256]{0:T(256)S(1)}, f32[256]{0:T(256)}, u32[]{:S(2)}) copy-start(f32[256]{0:T(256)} %param.32) | copy-start | bytes 3076
  102.4 115.3 %copy-start.108 = (f32[6]{0:T(128)S(1)}, f32[6]{0:T(128)}, u32[]{:S(2)}) copy-start(f32[6]{0:T(128)} %param.35) | copy-start | bytes 76
  102.5 115.4 %collective-permute-start = (bf16[3,640]{0,1:T(8,128)(2,1)S(1)}, bf16[3,640]{0,1:T(8,128)(2,1)S(1)}, u32[]{:S(2)}, u32[]{:S(2)}) collective-permute-start(bf16[3,640]{0,1:T(8,128)(2,1)S(1)} %pad_maximum_fusion.8), channel_id=1, source_target_pairs={{0,4},{4,8},{8,12},{1,5},{5,9},{9,13},{2,6},{6,10},{10,14},{3,7},{... | collective-permute-start | bytes 11528 | tf_op jit(solution)/shard_map/ppermute | solution.py:13
  105.3 112.5 %copy-start.78 = (f32[2,256]{1,0:T(2,128)}, f32[2,256]{1,0:T(2,128)S(1)}, u32[]{:S(2)}) copy-start(f32[2,256]{1,0:T(2,128)S(1)} %get-tuple-element.321) | copy-start | bytes 6148
  105.3 112.5 %copy-start.85 = (pred[2,256]{1,0:T(4,128)(4,1)}, pred[2,256]{1,0:T(4,128)(4,1)S(1)}, u32[]{:S(2)}) copy-start(pred[2,256]{1,0:T(4,128)(4,1)S(1)} %get-tuple-element.322) | copy-start | bytes 1540
  105.4 104.1 %copy-start.94 = (f32[2]{0:T(128)}, f32[2]{0:T(128)S(1)}, u32[]{:S(2)}) copy-start(f32[2]{0:T(128)S(1)} %compare_convert_fusion.1) | copy-start | bytes 28
  105.4 32.1 %copy-start.76 = (f32[512]{0:T(512)}, f32[512]{0:T(512)S(1)}, u32[]{:S(2)}) copy-start(f32[512]{0:T(512)S(1)} %convert_element_type.82) | copy-start | bytes 6148
  132.6 85.3 %copy-start.45 = (bf16[768,6]{0,1:T(8,128)(2,1)}, bf16[768,6]{0,1:T(8,128)(2,1)S(1)}, u32[]{:S(2)}) copy-start(bf16[768,6]{0,1:T(8,128)(2,1)S(1)} %reshape.360) | copy-start | bytes 27652
  133.5 199.2 %copy-start.41 = (f32[512,6]{0,1:T(8,128)}, f32[512,6]{0,1:T(8,128)S(1)}, u32[]{:S(2)}) copy-start(f32[512,6]{0,1:T(8,128)S(1)} %get-tuple-element.330) | copy-start | bytes 36868
  137.9 80.0 %copy-start.74 = (f32[2,6]{1,0:T(2,128)}, f32[2,6]{1,0:T(2,128)S(1)}, u32[]{:S(2)}) copy-start(f32[2,6]{1,0:T(2,128)S(1)} %slice_reduce_fusion) | copy-start | bytes 148
  139.0 79.2 %copy-start.56 = (f32[640]{0:T(1024)}, f32[640]{0:T(1024)S(1)}, u32[]{:S(2)}) copy-start(f32[640]{0:T(1024)S(1)} %get-tuple-element.259) | copy-start | bytes 7684
  139.0 79.2 %copy-start.58 = (f32[640]{0:T(1024)}, f32[640]{0:T(1024)S(1)}, u32[]{:S(2)}) copy-start(f32[640]{0:T(1024)S(1)} %get-tuple-element.260) | copy-start | bytes 7684
  139.0 79.2 %copy-start.60 = (f32[640]{0:T(1024)}, f32[640]{0:T(1024)S(1)}, u32[]{:S(2)}) copy-start(f32[640]{0:T(1024)S(1)} %get-tuple-element.261) | copy-start | bytes 7684
  139.1 79.2 %copy-start.62 = (f32[640]{0:T(1024)}, f32[640]{0:T(1024)S(1)}, u32[]{:S(2)}) copy-start(f32[640]{0:T(1024)S(1)} %get-tuple-element.262) | copy-start | bytes 7684
  174.8 43.5 %copy-start.66 = (f32[512]{0:T(512)S(1)}, f32[512]{0:T(512)}, u32[]{:S(2)}) copy-start(f32[512]{0:T(512)} %get-tuple-element.316) | copy-start | bytes 6148
  174.8 43.5 %copy-start.68 = (f32[512]{0:T(512)S(1)}, f32[512]{0:T(512)}, u32[]{:S(2)}) copy-start(f32[512]{0:T(512)} %get-tuple-element.317) | copy-start | bytes 6148
  174.8 43.5 %copy-start.70 = (f32[512]{0:T(512)S(1)}, f32[512]{0:T(512)}, u32[]{:S(2)}) copy-start(f32[512]{0:T(512)} %get-tuple-element.318) | copy-start | bytes 6148
  217.9 56.4 %copy-start.80 = (f32[384]{0:T(512)}, f32[384]{0:T(512)S(1)}, u32[]{:S(2)}) copy-start(f32[384]{0:T(512)S(1)} %mul.676) | copy-start | bytes 4612
  228.2 22.6 %copy-start.5 = (f32[2,256,6,64]{1,0,3,2:T(2,128)}, f32[2,256,6,64]{1,0,3,2:T(2,128)S(1)}, u32[]{:S(2)}) copy-start(f32[2,256,6,64]{1,0,3,2:T(2,128)S(1)} %reshape_reshape.6) | copy-start | bytes 2359300
  230.2 16.5 %copy-start.20 = (f32[2,6,64,128]{3,2,1,0:T(8,128)}, f32[2,6,64,128]{3,2,1,0:T(8,128)S(1)}, u32[]{:S(2)}) copy-start(f32[2,6,64,128]{3,2,1,0:T(8,128)S(1)} %fusion.49) | copy-start | bytes 1179652
  248.8 6.1 copy-start.40
  256.3 7.1 copy-start.64
  257.8 16.4 %copy-start.3 = (f32[512,384]{0,1:T(8,128)}, f32[512,384]{0,1:T(8,128)S(1)}, u32[]{:S(2)}) copy-start(f32[512,384]{0,1:T(8,128)S(1)} %get-tuple-element.300) | copy-start | bytes 2359300
  263.5 10.8 %copy-start.54 = (f32[512]{0:T(512)}, f32[512]{0:T(512)S(1)}, u32[]{:S(2)}) copy-start(f32[512]{0:T(512)S(1)} %add_rsqrt_fusion) | copy-start | bytes 6148
  284.2 7.4 %copy-start.8 = (f32[2,256,6,64]{1,0,3,2:T(2,128)S(1)}, f32[2,256,6,64]{1,0,3,2:T(2,128)}, u32[]{:S(2)}) copy-start(f32[2,256,6,64]{1,0,3,2:T(2,128)} %reshape_reshape.7) | copy-start | bytes 2359300
  284.2 7.4 %copy-start.36 = (f32[2,256,128,1]{2,1,3,0:T(8,128)S(1)}, f32[2,256,128,1]{2,1,3,0:T(8,128)}, u32[]{:S(2)}) copy-start(f32[2,256,128,1]{2,1,3,0:T(8,128)} %copy.337) | copy-start | bytes 786436
  284.2 8.2 %copy-start.98 = (f32[6]{0:T(128)S(1)}, f32[6]{0:T(128)}, u32[]{:S(2)}) copy-start(f32[6]{0:T(128)} %get-tuple-element.323) | copy-start | bytes 76
  292.4 21.2 %copy-start.27 = (f32[2,6,64,128]{3,2,1,0:T(8,128)}, f32[2,6,64,128]{3,2,1,0:T(8,128)S(1)}, u32[]{:S(2)}) copy-start(f32[2,6,64,128]{3,2,1,0:T(8,128)S(1)} %fusion.46) | copy-start | bytes 1179652
  326.8 5.9 copy-start.10
  332.6 105.4 %reduce-scatter.16.cloned.1.call-start = ((), (), s32[]{:S(2)}) async-start(), calls=%async_computation.11 | async-start | bytes 442368
  337.7 17.7 %copy-start.52 = (f32[2,256,6]{1,2,0:T(8,128)S(1)}, f32[2,256,6]{1,2,0:T(8,128)}, u32[]{:S(2)}) copy-start(f32[2,256,6]{1,2,0:T(8,128)} %multiply_reduce_fusion.11) | copy-start | bytes 36868
  337.7 17.7 %copy-start.79 = (f32[2,256]{1,0:T(2,128)S(1)}, f32[2,256]{1,0:T(2,128)}, u32[]{:S(2)}) copy-start(f32[2,256]{1,0:T(2,128)} %copy-done.78) | copy-start | bytes 6148
  337.8 33.9 %copy-start.19 = (bf16[512,384]{0,1:T(8,128)(2,1)S(1)}, bf16[512,384]{0,1:T(8,128)(2,1)}, u32[]{:S(2)}) copy-start(bf16[512,384]{0,1:T(8,128)(2,1)} %get-tuple-element.303) | copy-start | bytes 1179652
  337.8 33.9 %copy-start.31 = (bf16[768,384]{1,0:T(8,128)(2,1)S(1)}, bf16[768,384]{1,0:T(8,128)(2,1)}, u32[]{:S(2)}) copy-start(bf16[768,384]{1,0:T(8,128)(2,1)} %all_gather.50) | copy-start | bytes 1769476
  339.7 35.2 %copy-start.53 = (f32[512,6]{0,1:T(8,128)S(1)}, f32[512,6]{0,1:T(8,128)}, u32[]{:S(2)}) copy-start(f32[512,6]{0,1:T(8,128)} %get-tuple-element.331) | copy-start | bytes 36868
  339.7 35.2 %copy-start.77 = (f32[512]{0:T(512)S(1)}, f32[512]{0:T(512)}, u32[]{:S(2)}) copy-start(f32[512]{0:T(512)} %copy-done.76) | copy-start | bytes 6148
  378.3 61.3 %all-reduce.18.cloned.1.call-start = ((), (), s32[]{:S(2)}) async-start(), calls=%async_computation.6 | async-start | bytes 3145728 | tf_op jit(solution)/shard_map/psum | solution.py:295
  383.4 9.6 %collective-permute-start.1 = (f32[3,640]{0,1:T(8,128)S(1)}, f32[3,640]{0,1:T(8,128)S(1)}, u32[]{:S(2)}, u32[]{:S(2)}) collective-permute-start(f32[3,640]{0,1:T(8,128)S(1)} %pad_add_fusion.1), channel_id=1, source_target_pairs={{4,0},{8,4},{12,8},{5,1},{9,5},{13,9},{6,2},{10,6},{14,10},{7,3},{... | collective-permute-start | bytes 23048 | tf_op jit(solution)/shard_map/ppermute | solution.py:13
  386.1 7.5 %copy-start.26 = (bf16[768,256]{1,0:T(8,128)(2,1)S(1)}, bf16[768,256]{1,0:T(8,128)(2,1)}, u32[]{:S(2)}) copy-start(bf16[768,256]{1,0:T(8,128)(2,1)} %copy-done.25) | copy-start | bytes 1179652
  393.5 6.9 copy-start.16
  397.2 89.1 %all-gather.5.cloned.1.call-start = ((), (), s32[]{:S(2)}) async-start(), calls=%async_computation.10 | async-start | bytes 7864320 | tf_op jit(solution)/shard_map/all_gather | solution.py:215
  400.4 103.8 %reduce-scatter.14.cloned.1.call-start = ((), (), s32[]{:S(2)}) async-start(), calls=%async_computation.9 | async-start | bytes 884736 | tf_op jit(solution)/shard_map/reduce_scatter | solution.py:307
  401.8 170.0 %reduce-scatter.10.cloned.1.call-start = ((), (), s32[]{:S(2)}) async-start(), calls=%async_computation.7 | async-start | bytes 1327104 | tf_op jit(solution)/shard_map/reduce_scatter | solution.py:305
  403.6 235.9 %reduce-scatter.18.cloned.1.call-start = ((), (), s32[]{:S(2)}) async-start(), calls=%async_computation.12 | async-start | bytes 1327104
  408.0 31.5 %copy-start.84 = (f32[640]{0:T(1024)S(1)}, f32[640]{0:T(1024)}, u32[]{:S(2)}) copy-start(f32[640]{0:T(1024)} %get-tuple-element.251) | copy-start | bytes 7684
  408.0 31.5 %copy-start.83 = (f32[640]{0:T(1024)S(1)}, f32[640]{0:T(1024)}, u32[]{:S(2)}) copy-start(f32[640]{0:T(1024)} %get-tuple-element.250) | copy-start | bytes 7684
  408.0 31.5 %copy-start.82 = (f32[640]{0:T(1024)S(1)}, f32[640]{0:T(1024)}, u32[]{:S(2)}) copy-start(f32[640]{0:T(1024)} %get-tuple-element.249) | copy-start | bytes 7684
  408.0 31.6 %copy-start.1 = (f32[512,768]{1,0:T(8,128)S(1)}, f32[512,768]{1,0:T(8,128)}, u32[]{:S(2)}) copy-start(f32[512,768]{1,0:T(8,128)} %param.22) | copy-start | bytes 4718596
  408.0 31.6 %copy-start.51 = (f32[768]{0:T(1024)S(1)}, f32[768]{0:T(1024)}, u32[]{:S(2)}) copy-start(f32[768]{0:T(1024)} %copy-done.50) | copy-start | bytes 9220
  408.1 31.6 %copy-start.73 = (f32[512]{0:T(512)S(1)}, f32[512]{0:T(512)}, u32[]{:S(2)}) copy-start(f32[512]{0:T(512)} %copy-done.72) | copy-start | bytes 6148
  408.1 299.1 %reduce-scatter.12.cloned.1.call-start = ((), (), s32[]{:S(2)}) async-start(), calls=%async_computation.8 | async-start | bytes 1327104 | tf_op jit(solution)/shard_map/reduce_scatter | solution.py:306
  (59 other events, 163.2 us)
Sparse Core Ops, SparseCore 0:
  332.7 30.6 all-reduce.15
  397.4 40.3 all-reduce.17
  439.9 46.4 all-gather.4
Sparse Core Ops, SparseCore 1:
  378.4 59.5 reduce-scatter.15
  441.7 62.4 reduce-scatter.13
  508.0 63.7 reduce-scatter.9
  575.8 63.7 reduce-scatter.17
  643.5 63.6 reduce-scatter.11
